TPU v7x, 512 devices: a whole 4x8x8 slice. The times are simulated.
512 devices in a mesh: date: 16 (over z, x_hi), trade: 16 (over y, core), path: 2 (over x_lo).
Axes of the slice: x: 4 (x_hi: 2, x_lo: 2; x = x_hi * 2 + x_lo), y: 8, z: 8, core: 2. Of those that a mesh axis runs over, the one named last changes fastest.
Arguments:
- normals: bfloat16 [32, 64, 8192], P('date', None, ('trade', 'path')), may hold values from -6 to 6
- chol: float32 [64, 64], replicated, as said below
- volatility: float32 [64], replicated, may hold values from 0.5 to 2
- start_state: float32 [64], replicated, may hold values from -3 to 3
- basis_map: float32 [64, 128], replicated, may hold values from -0.75 to 0.75
- basis_bias: float32 [128], replicated, may hold values from -3 to 3
- coef: bfloat16 [128, 16384], P(None, 'trade'), may hold values from -0.5 to 0.5
- maturity: int32 [16384], P('trade'), may hold values from 1 to 32
- netting: int32 [16384], P('trade'), may hold values from 0 to 2047, as said below
Outputs:
- exposure: float32 [32, 2048], P('date', 'trade')
Inputs may be any that keep to these rules, and one draw needn't show every extreme that they name: netting sets are whole within a shard of trades: netting[j] // 128 == j // 1024, and every netting set holds at least one trade. `chol`: lower triangular with a positive diagonal.
All inputs are finite; a program needn't handle non-finite values.
Results may differ from a plain program's by a relative error of at most 0.00035.
Values may be sent and summed in bfloat16 or wider, within the bound.
A program may use at most 64 MiB of HBM per device.

v0:
```python
import jax
import jax.numpy as jnp
from jax import lax
from jax.sharding import PartitionSpec as P

NS_DEV = 128


def entering(array, axis, join, neutral):
    place = lax.axis_index(axis)
    gathered = lax.all_gather(array.astype(jnp.bfloat16), axis)
    state = jnp.zeros_like(array) + jnp.asarray(neutral, array.dtype)

    def one(lap, state):
        return join(state, lax.dynamic_index_in_dim(gathered, lap, 0, False).astype(array.dtype))

    return lax.fori_loop(0, place, one, state)


def add_pair(earlier, later):
    return earlier + later


def local_moves(draws, chol, volatility, date_total):
    scale = volatility * jnp.sqrt(jnp.float32(1.0) / date_total)
    moves = jnp.einsum(
        "fg,tgp->tfp", chol, draws.astype(jnp.float32), precision=lax.Precision.HIGHEST
    )
    return jnp.cumsum(moves * scale[None, :, None], axis=0)


def shards(normals, chol, volatility, start_state, basis_map, basis_bias, coef, maturity, netting):
    date_count, factor_count, path_count = normals.shape
    trade_count = coef.shape[1]
    set_count = trade_count * 0 + NS_DEV
    date_total = date_count * lax.axis_size("date")
    path_total = path_count * lax.axis_size("trade") * lax.axis_size("path")
    first_date = lax.axis_index("date") * date_count
    when = first_date + jnp.arange(date_count, dtype=jnp.int32)
    alive = (when[:, None] < maturity[None, :]).astype(jnp.float32)
    local_set = netting - lax.axis_index("trade") * set_count
    member = (local_set[:, None] == jnp.arange(set_count, dtype=jnp.int32)[None, :]).astype(
        jnp.bfloat16
    )
    own_local = local_moves(normals, chol, volatility, date_total)
    empty = jnp.zeros_like(own_local[-1])
    prior = entering(own_local[-1], "date", add_pair, empty)
    states = start_state[None, :, None] + prior[None] + own_local
    pre = jnp.einsum(
        "tfp,fk->tpk",
        lax.all_gather(states, "trade", axis=2, tiled=True),
        basis_map,
        precision=lax.Precision.HIGHEST,
    )
    basis = jnp.tanh(pre + basis_bias[None, None, :]).astype(jnp.bfloat16)
    value = jnp.einsum("tpk,kj->tpj", basis, coef, preferred_element_type=jnp.float32)
    value = (value * alive[:, None, :]).astype(jnp.bfloat16)
    net = jnp.einsum("tpj,js->tps", value, member, preferred_element_type=jnp.float32)
    total = jnp.sum(jnp.maximum(net, 0.0), axis=1)
    summed = lax.psum(total, "path")
    return summed / path_total


def solution(mesh):
    placed = (
        P("date", None, ("trade", "path")),
        P(),
        P(),
        P(),
        P(),
        P(),
        P(None, "trade"),
        P("trade"),
        P("trade"),
    )
    return jax.shard_map(
        shards, mesh=mesh, in_specs=placed, out_specs=P("date", "trade"), check_vma=False
    )
```

profile of v0, /device:TPU:1, one launch (start us, length us, event | category | flops | bytes accessed | tf_op | source)
XLA Modules:
  0.0 125.8 jit_solution(15111759457493451321)
XLA Ops:
  6.5 0.0 copy-start
  6.5 0.0 copy-start.4
  6.5 0.0 copy-start.3
  6.5 0.0 copy-start.2
  6.5 0.0 copy-start.1
  6.5 0.0 copy-start.5
  6.6 0.0 all-gather.2.cloned.1.call-start
  6.6 0.7 broadcast_multiply_fusion.1
  7.3 1.0 fusion.8
  8.4 0.1 fusion.16
  8.5 43.9 %all_gather.7 = bf16[16,64,256]{2,1,0:T(8,128)(2,1)S(1)} all-gather(bf16[1,64,256]{2,1,0:T(8,128)(2,1)S(1)} %slice.7), channel_id=1, replica_groups=mesh['date'=16,'trade'=16,'path'=2] {'date'}, dimensions={0}, use_global_device_ids=true | all-gather | bytes 557056 | tf_op jit(solution)/shard_map/all_gather | solution.py:11
  52.4 0.0 copy-done.4
  52.4 0.1 broadcast_add_fusion.1
  52.5 0.7 broadcast_add_fusion
  53.2 0.0 all-gather.2.cloned.1.call-update
  53.2 0.0 copy-done.3
  53.2 0.0 copy-done.2
  53.2 0.1 compare_convert_fusion
  53.3 43.9 %all-gather.2.cloned.1.call-done = f32[2,64,4096]{2,1,0:T(8,128)} async-done(((f32[2,64,256]{2,1,0:T(8,128)}), f32[2,64,4096]{2,1,0:T(8,128)}) %all-gather.2.cloned.1.call-update) | async-done | bytes 2097168 | tf_op jit(solution)/shard_map/all_gather | solution.py:51
  97.2 0.0 copy-done.1
  97.2 0.0 copy-done.5
  97.2 8.3 %fusion.6 = bf16[2,4096,128]{2,1,0:T(8,128)(2,1)S(1)} fusion(f32[2,64,4096]{2,1,0:T(8,128)} %all-gather.2.cloned.1.call-done, f32[128]{0:T(128)S(1)} %copy-done.5, f32[64,128]{1,0:T(8,128)S(1)} %copy-done.1), kind=kOutput, calls=%fused_computation.8 | convolution fusion | flops 807403520 | bytes 4227584 | tf_op jit(solution)/shard_map/tfp,fk->tpk/dot_general | solution.py:49
  105.5 0.0 copy-done
  105.5 9.0 %fusion.7 = f32[2,128]{1,0:T(2,128)S(1)} fusion(f32[2,1024]{1,0:T(2,128)S(1)} %compare_convert_fusion, bf16[2,4096,128]{2,1,0:T(8,128)(2,1)S(1)} %fusion.6, bf16[128,1024]{1,0:T(8,128)(2,1)S(1)} %copy-done, s32[1024]{0:T(1024)S(1)} %broadcast_subtract_fusion), kind=kOutput, calls=%fused_computation.9 | convolution fusion | flops 4313972736 | bytes 2372608 | tf_op jit(solution)/shard_map/tpj,js->tps/dot_general | solution.py:58
  114.6 3.8 %psum.7 = f32[2,128]{1,0:T(2,128)S(1)} all-reduce(f32[2,128]{1,0:T(2,128)S(1)} %fusion.7), channel_id=1, replica_groups=mesh['date'=16,'trade'=16,'path'=2] {'path'}, use_global_device_ids=true, to_apply=%region_4.5 | all-reduce | flops 256 | bytes 2048 | tf_op jit(solution)/shard_map/psum | solution.py:60
  118.3 0.6 broadcast_multiply_fusion
  (5 shorter events, 0.0 us)
Async XLA Ops:
  6.5 99.0 %copy-start = (bf16[128,1024]{1,0:T(8,128)(2,1)S(1)}, bf16[128,1024]{1,0:T(8,128)(2,1)}, u32[]{:S(2)}) copy-start(bf16[128,1024]{1,0:T(8,128)(2,1)} %param.17) | copy-start | bytes 786436
  6.5 45.9 %copy-start.4 = (f32[64]{0:T(128)S(1)}, f32[64]{0:T(128)}, u32[]{:S(2)}) copy-start(f32[64]{0:T(128)} %param.14) | copy-start | bytes 772
  6.5 46.7 %copy-start.3 = (s32[1024]{0:T(1024)S(1)}, s32[1024]{0:T(1024)}, u32[]{:S(2)}) copy-start(s32[1024]{0:T(1024)} %param.19) | copy-start | bytes 12292
  6.5 46.7 %copy-start.2 = (s32[1024]{0:T(1024)S(1)}, s32[1024]{0:T(1024)}, u32[]{:S(2)}) copy-start(s32[1024]{0:T(1024)} %param.18) | copy-start | bytes 12292
  6.5 90.6 %copy-start.1 = (f32[64,128]{1,0:T(8,128)S(1)}, f32[64,128]{1,0:T(8,128)}, u32[]{:S(2)}) copy-start(f32[64,128]{1,0:T(8,128)} %param.15) | copy-start | bytes 98308
  6.5 90.6 %copy-start.5 = (f32[128]{0:T(128)S(1)}, f32[128]{0:T(128)}, u32[]{:S(2)}) copy-start(f32[128]{0:T(128)} %param.16) | copy-start | bytes 1540
  6.6 90.6 %all-gather.2.cloned.1.call-start = ((), (), s32[]{:S(2)}) async-start(), calls=%async_computation | async-start | bytes 2228224 | tf_op jit(solution)/shard_map/all_gather | solution.py:51
Sparse Core Ops, SparseCore 0:
  53.3 43.8 all-gather.1
where the time goes:
time: 126 us
  blocking collectives  47.7 us (38%)
  waiting for transfers between devices  43.9 us (35%)
  matrix products  18.4 us (15%)
  between operations  13.5 us (11%)
  other arithmetic  2.22 us (2%)
    all_gather x1, blocking collectives, entering(): gathered = lax.all_gather(array.astype(jnp.bfloat16), axis)  43.9 us
    all_gather x1, waiting for transfers between devices, shards(): lax.all_gather(states, 'trade', axis=2, tiled=True)  43.9 us
    dot_general x1, matrix products, shards(): jnp.einsum('tpj,js->tps', value, member, preferred_element_type=jnp.float32)  9.03 us
    dot_general x1, matrix products, shards(): jnp.einsum('tfp,fk->tpk', lax.all_gather(states, 'trade', axis=2, tiled=T...  8.32 us
    psum x1, blocking collectives, shards(): summed = lax.psum(total, 'path')  3.79 us
  transfers between devices with their start and end apart: 1, of which 1 were waited for; matrix products, arithmetic and copies ran while one was open for 0% of the time, Pallas kernels for 0%

commit v1 on v0

--- a/solution.py
+++ b/solution.py
@@ -4,6 +4,12 @@
 from jax.sharding import PartitionSpec as P
 
 NS_DEV = 128
+load_the_strings = lambda panel: jnp.concatenate(
+    lax.all_to_all(
+        jnp.stack([panel] * lax.psum(1, axis_name="trade")), "trade", split_axis=0, concat_axis=0
+    ),
+    axis=2,
+)
 
 
 def entering(array, axis, join, neutral):
@@ -47,10 +53,7 @@
     prior = entering(own_local[-1], "date", add_pair, empty)
     states = start_state[None, :, None] + prior[None] + own_local
     pre = jnp.einsum(
-        "tfp,fk->tpk",
-        lax.all_gather(states, "trade", axis=2, tiled=True),
-        basis_map,
-        precision=lax.Precision.HIGHEST,
+        "tfp,fk->tpk", load_the_strings(states), basis_map, precision=lax.Precision.HIGHEST
     )
     basis = jnp.tanh(pre + basis_bias[None, None, :]).astype(jnp.bfloat16)
     value = jnp.einsum("tpk,kj->tpj", basis, coef, preferred_element_type=jnp.float32)

time: 126 us -> 133 us (1.056)
  starting transfers between devices: 0.04 us -> 14.7 us
  between operations: 13.5 us -> 0.1 us
  waiting for transfers between devices: 43.9 us -> 48.8 us
  local copies, waits for them, and re-layouts: 0.03 us -> 2.36 us
    all_to_all x0 -> x1, waiting for transfers between devices: none -> 48.8 us  [lax.all_to_all(jnp.stack([panel] * lax.psum(1, axis_name='trade')), 'trad...]
    all_gather x1 -> x0, waiting for transfers between devices: 43.9 us -> none  [shards(): lax.all_gather(states, 'trade', axis=2, tiled=True)]
    all_to_all x0 -> x1, starting transfers between devices: none -> 14.7 us  [lax.all_to_all(jnp.stack([panel] * lax.psum(1, axis_name='trade')), 'trad...]
    another operation x0 -> x1, local copies, waits for them, and re-layouts: none -> 1.58 us  [jnp.stack([panel] * lax.psum(1, axis_name='trade'))]
where the time goes in v1:
time: 133 us; the launch traced here: 132 us
  waiting for transfers between devices  48.8 us (37%)
  blocking collectives  47.7 us (36%)
  matrix products  17.2 us (13%)
  starting transfers between devices  14.7 us (11%)
  local copies, waits for them, and re-layouts  2.36 us (2%)
  other arithmetic  1.57 us (1%)
    all_to_all x1, waiting for transfers between devices, lax.all_to_all(jnp.stack([panel] * lax.psum(1, axis_name='trade')), 'trad...  48.8 us
    all_gather x1, blocking collectives, entering(): gathered = lax.all_gather(array.astype(jnp.bfloat16), axis)  43.9 us
    all_to_all x1, starting transfers between devices, lax.all_to_all(jnp.stack([panel] * lax.psum(1, axis_name='trade')), 'trad...  14.7 us
    dot_general x1, matrix products, shards(): jnp.einsum('tpj,js->tps', value, member, preferred_element_type=jnp.float32)  9.03 us
    dot_general x1, matrix products, shards(): jnp.einsum('tfp,fk->tpk', load_the_strings(states), basis_map, precision=...  7.17 us
    psum x1, blocking collectives, shards(): summed = lax.psum(total, 'path')  3.79 us
  transfers between devices with their start and end apart: 1, of which 1 were waited for; matrix products, arithmetic and copies ran while one was open for 0% of the time, Pallas kernels for 0%

profile of v1, /device:TPU:1, one launch (start us, length us, event | category | flops | bytes accessed | tf_op | source)
XLA Modules:
  0.0 132.5 jit_solution(4525927525476200663)
XLA Ops:
  0.0 0.0 copy-start
  0.0 0.0 copy-start.4
  0.0 0.7 broadcast_multiply_fusion.1
  0.7 1.0 fusion.8
  1.8 0.1 fusion.16
  1.9 43.9 %all_gather.4 = bf16[16,64,256]{2,1,0:T(8,128)(2,1)S(1)} all-gather(bf16[1,64,256]{2,1,0:T(8,128)(2,1)S(1)} %slice.7), channel_id=1, replica_groups=mesh['date'=16,'trade'=16,'path'=2] {'date'}, dimensions={0}, use_global_device_ids=true | all-gather | bytes 557056 | tf_op jit(solution)/shard_map/all_gather | solution.py:17
  45.8 0.0 copy-done.4
  45.8 0.1 broadcast_add_fusion.1
  45.9 1.6 %stack.2 = f32[16,2,64,256]{3,2,1,0:T(8,128)} broadcast(f32[2,64,256]{2,1,0:T(8,128)S(1)} %broadcast_add_fusion), dimensions={1,2,3} | broadcast | bytes 2228224 | tf_op jit(solution)/shard_map/stack | solution.py:9
  47.5 0.0 copy-start.3
  47.5 0.0 copy-start.2
  47.5 14.7 %all-to-all-start = ((f32[16,2,64,256]{3,2,1,0:T(8,128)}), f32[16,2,64,256]{3,2,1,0:T(8,128)S(1)}, u32[]{:S(2)}, u32[]{:S(2)}) async-start(f32[16,2,64,256]{3,2,1,0:T(8,128)} %stack.2), calls=%async_computation | async-start | bytes 4194304 | tf_op jit(solution)/shard_map/all_to_all | solution.py:8
  62.2 0.0 copy-done.3
  62.2 0.0 copy-done.2
  62.2 0.1 compare_convert_fusion
  62.3 48.8 %all-to-all-done = f32[16,2,64,256]{3,2,1,0:T(8,128)S(1)} async-done(((f32[16,2,64,256]{3,2,1,0:T(8,128)}), f32[16,2,64,256]{3,2,1,0:T(8,128)S(1)}, u32[]{:S(2)}, u32[]{:S(2)}) %all-to-all-start) | async-done | bytes 2097184 | tf_op jit(solution)/shard_map/all_to_all | solution.py:8
  111.1 0.0 copy-start.1
  111.1 0.0 copy-start.5
  111.1 0.2 copy.11
  111.3 0.6 copy-done.1
  111.9 0.0 copy-done.5
  111.9 7.2 %fusion.6 = bf16[2,4096,128]{2,1,0:T(8,128)(2,1)S(1)} fusion(f32[2,64,4096]{2,1,0:T(8,128)S(1)} %bitcast.28, f32[128]{0:T(128)S(1)} %copy-done.5, f32[64,128]{1,0:T(8,128)S(1)} %copy-done.1), kind=kOutput, calls=%fused_computation.8 | convolution fusion | flops 807403520 | bytes 4227584 | tf_op jit(solution)/shard_map/tfp,fk->tpk/dot_general | solution.py:55
  119.1 0.0 copy-done
  119.1 9.0 %fusion.7 = f32[2,128]{1,0:T(2,128)S(1)} fusion(f32[2,1024]{1,0:T(2,128)S(1)} %compare_convert_fusion, bf16[2,4096,128]{2,1,0:T(8,128)(2,1)S(1)} %fusion.6, bf16[128,1024]{1,0:T(8,128)(2,1)S(1)} %copy-done, s32[1024]{0:T(1024)S(1)} %broadcast_subtract_fusion), kind=kOutput, calls=%fused_computation.9 | convolution fusion | flops 4313972736 | bytes 2372608 | tf_op jit(solution)/shard_map/tpj,js->tps/dot_general | solution.py:61
  128.1 3.8 %psum.7 = f32[2,128]{1,0:T(2,128)S(1)} all-reduce(f32[2,128]{1,0:T(2,128)S(1)} %fusion.7), channel_id=1, replica_groups=mesh['date'=16,'trade'=16,'path'=2] {'path'}, use_global_device_ids=true, to_apply=%region_4.5 | all-reduce | flops 256 | bytes 2048 | tf_op jit(solution)/shard_map/psum | solution.py:63
  131.9 0.6 broadcast_multiply_fusion
  (6 shorter events, 0.0 us)
Async XLA Ops:
  0.0 119.1 %copy-start = (bf16[128,1024]{1,0:T(8,128)(2,1)S(1)}, bf16[128,1024]{1,0:T(8,128)(2,1)}, u32[]{:S(2)}) copy-start(bf16[128,1024]{1,0:T(8,128)(2,1)} %param.17) | copy-start | bytes 786436
  0.0 45.8 %copy-start.4 = (f32[64]{0:T(128)S(1)}, f32[64]{0:T(128)}, u32[]{:S(2)}) copy-start(f32[64]{0:T(128)} %param.14) | copy-start | bytes 772
  47.5 14.7 %copy-start.3 = (s32[1024]{0:T(1024)S(1)}, s32[1024]{0:T(1024)}, u32[]{:S(2)}) copy-start(s32[1024]{0:T(1024)} %param.19) | copy-start | bytes 12292
  47.5 14.7 %copy-start.2 = (s32[1024]{0:T(1024)S(1)}, s32[1024]{0:T(1024)}, u32[]{:S(2)}) copy-start(s32[1024]{0:T(1024)} %param.18) | copy-start | bytes 12292
  47.5 63.6 %all-to-all-start = ((f32[16,2,64,256]{3,2,1,0:T(8,128)}), f32[16,2,64,256]{3,2,1,0:T(8,128)S(1)}, u32[]{:S(2)}, u32[]{:S(2)}) async-start(f32[16,2,64,256]{3,2,1,0:T(8,128)} %stack.2), calls=%async_computation | async-start | bytes 4194304 | tf_op jit(solution)/shard_map/all_to_all | solution.py:8
  111.1 0.8 copy-start.1
  111.1 0.8 copy-start.5
